TPU v7x, 128 devices: a whole 4x4x4 slice. The times are simulated.
128 devices in a mesh: section: 8 (over y_hi, z), seq: 16 (over x, y_lo, core).
Axes of the slice: x: 4, y: 4 (y_hi: 2, y_lo: 2; y = y_hi * 2 + y_lo), z: 4, core: 2. Of those that a mesh axis runs over, the one named last changes fastest.
Arguments:
- inbound_embedding_batches: bfloat16 [2, 128, 4096], replicated, may hold values from -16 to 16
- decoder_embedding_batches: bfloat16 [2, 128, 4096], replicated, may hold values from -16 to 16
- asking_projections: bfloat16 [8, 4096, 4096], P('section', None, 'seq'), may hold values from -0.09375 to 0.09375
- probe_projections: bfloat16 [8, 4096, 4096], P('section', None, 'seq'), may hold values from -0.09375 to 0.09375
- payload_projections: bfloat16 [8, 4096, 4096], P('section', None, 'seq'), may hold values from -0.09375 to 0.09375
- exit_projections: bfloat16 [8, 4096, 4096], P('section', 'seq'), may hold values from -0.1875 to 0.1875
- layer_rescale_weights: float32 [8, 4096], P('section'), may hold values from 0.1 to 1.9
- logit_sharpness: float32 [8, 64], P('section', 'seq'), may hold values from 0.5 to 3
- last_rescale_weights: float32 [4096], replicated, may hold values from 0.1 to 1.9
Outputs:
- section_out: bfloat16 [8, 2, 128, 4096], P('section')
All inputs are finite; a program needn't handle non-finite values.
Results may differ from a plain program's by a relative error of at most 0.025.
Values may be sent and summed in bfloat16 or wider, within the bound.
A program may use at most 64 MiB of HBM per device.

v0:
```python
import math
import jax
import jax.numpy as jnp
from jax import lax
from jax.sharding import PartitionSpec as P

epsilon = 1e-06


def from_behind(x, axis, by):
    count = lax.axis_size(axis)
    pairs = [(i, i + by) for i in range(count) if 0 <= i + by < count]
    return lax.ppermute(x, axis, pairs)


def broadcast(value, axis, source):
    kept = jnp.where(lax.axis_index(axis) == source, value, 0).astype(value.dtype)
    return lax.psum(kept, axis)


def normalize(row_block, gain_vector):
    values = row_block.astype(jnp.float32)
    factor = lax.rsqrt(jnp.mean(values * values, axis=-1, keepdims=True) + epsilon)
    return (values * factor * gain_vector).astype(jnp.bfloat16)


def unit_heads(projected):
    return (
        projected * lax.rsqrt(jnp.mean(projected * projected, axis=-1, keepdims=True) + epsilon)
    ).astype(jnp.bfloat16)


def attend(queries, keys_proj, values_proj, logit_divisor):
    length = queries.shape[0]
    key_length = keys_proj.shape[0]
    head_count = logit_divisor.shape[0]
    head_size = queries.shape[1] // head_count
    unit_query = unit_heads(queries.reshape(length, head_count, head_size))
    unit_key = unit_heads(keys_proj.reshape(key_length, head_count, head_size))
    values = values_proj.astype(jnp.bfloat16).reshape(key_length, head_count, head_size)
    scores = jnp.einsum("qhd,khd->hqk", unit_query, unit_key, preferred_element_type=jnp.float32)
    scores = scores * (logit_divisor[:, None, None] / math.sqrt(head_size))
    weights = jnp.exp(scores)
    weights = (weights / jnp.sum(weights, axis=-1, keepdims=True)).astype(jnp.bfloat16)
    blended_payloads = jnp.einsum(
        "hqk,khd->qhd", weights, values, preferred_element_type=jnp.float32
    )
    return blended_payloads.astype(jnp.bfloat16).reshape(length, head_count * head_size)


def shards(
    inbound_embedding_batches,
    decoder_embedding_batches,
    asking_projections,
    probe_projections,
    payload_projections,
    exit_projections,
    layer_rescale_weights,
    logit_sharpness,
    last_rescale_weights,
):
    section_count = lax.axis_size("section")
    seq_count = lax.axis_size("seq")
    present_layer_index = lax.axis_index("section")
    seq_index = lax.axis_index("seq")
    encoders = 3 * section_count // 8
    batches = inbound_embedding_batches.shape[0]
    length = inbound_embedding_batches.shape[1]
    width = inbound_embedding_batches.shape[2]
    share_rows = length // seq_count
    first_own = seq_index * share_rows
    ticks = section_count + batches - 1
    w_query = asking_projections[0]
    w_key = probe_projections[0]
    w_value = payload_projections[0]
    w_output = exit_projections[0]
    logit_divisor = logit_sharpness[0]
    gain_vector = layer_rescale_weights[0]
    is_encoder = present_layer_index < encoders

    def layer(stream, memory_raw):
        rescaled_activations = normalize(stream, gain_vector)
        remote = normalize(memory_raw, last_rescale_weights)
        source_kv = jnp.where(is_encoder, rescaled_activations, remote)
        queries = jnp.dot(rescaled_activations, w_query, preferred_element_type=jnp.float32)
        keys_proj = jnp.dot(source_kv, w_key, preferred_element_type=jnp.float32)
        values_proj = jnp.dot(source_kv, w_value, preferred_element_type=jnp.float32)
        blended_payloads = attend(queries, keys_proj, values_proj, logit_divisor)
        update = lax.psum_scatter(
            jnp.dot(blended_payloads, w_output, preferred_element_type=jnp.float32).astype(
                jnp.bfloat16
            ),
            "seq",
            scatter_dimension=0,
            tiled=True,
        ).astype(jnp.float32)
        own_rows = lax.dynamic_slice_in_dim(stream, first_own, share_rows, 0)
        return (own_rows.astype(jnp.float32) + update).astype(jnp.bfloat16)

    blank = jnp.zeros((length, width), inbound_embedding_batches.dtype)
    holder = jnp.zeros((batches,) + blank.shape, inbound_embedding_batches.dtype)

    def advance(tick_index, state_tuple):
        arrived, carried, stored, finished = state_tuple
        offset = tick_index - present_layer_index
        batch_index = jnp.clip(offset, 0, batches - 1)
        valid = (offset >= 0) & (offset < batches)
        source_rows = lax.dynamic_index_in_dim(
            inbound_embedding_batches, batch_index, 0, keepdims=False
        )
        target_rows = lax.dynamic_index_in_dim(
            decoder_embedding_batches, batch_index, 0, keepdims=False
        )
        memory_kept = lax.dynamic_index_in_dim(stored, batch_index, 0, keepdims=False)
        arrived_rows = arrived
        stream = jnp.where(
            present_layer_index == 0,
            source_rows,
            jnp.where(present_layer_index == encoders, target_rows, arrived_rows),
        )
        share = layer(stream, memory_kept)
        outgoing = lax.all_gather(share, "seq", axis=0, tiled=True)
        written = lax.dynamic_update_index_in_dim(finished, outgoing, batch_index, 0)
        finished = jnp.where(valid, written, finished)
        arrived = from_behind(outgoing, "section", 1)
        encoded = broadcast(outgoing, "section", encoders - 1)
        produced = tick_index - (encoders - 1)
        ready = (produced >= 0) & (produced < batches)
        placed = lax.dynamic_update_index_in_dim(
            stored, encoded, jnp.clip(produced, 0, batches - 1), 0
        )
        stored = jnp.where(ready, placed, stored)
        return (arrived, carried, stored, finished)

    final_state = lax.fori_loop(0, ticks, advance, (blank, blank, holder, holder))
    finished = final_state[3]
    return finished[None]


def solution(mesh):
    return jax.shard_map(
        shards,
        mesh=mesh,
        in_specs=(
            P(),
            P(),
            P("section", None, "seq"),
            P("section", None, "seq"),
            P("section", None, "seq"),
            P("section", "seq", None),
            P("section", None),
            P("section", "seq"),
            P(),
        ),
        out_specs=P("section", None, None, None),
        check_vma=False,
    )
```

profile of v0, /device:TPU:0, one launch (start us, length us, event | category | flops | bytes accessed | tf_op | source)
XLA Modules:
  0.0 1826.0 jit_solution(14866793786622618340)
XLA Ops:
  9.4 1809.7 %while.19 = (s32[]{:T(128)}, bf16[128,4096]{1,0:T(8,128)(2,1)}, bf16[2,128,4096]{2,1,0:T(8,128)(2,1)S(1)}, bf16[2,128,4096]{2,1,0:T(8,128)(2,1)}, pred[]{:T(512)...) while((s32[]{:T(128)}, bf16[128,4096]{1,0:T(8,128)(2,1)}, ...), condition=%wide.region_8.9_spmd, body=%wide.region_0.8_spmd.sunk | while | flops 1104807808 | bytes 77665632 | solution.py:135
  10.1 2.8 fusion.48
  21.4 3.0 convolution_convert_fusion.8
  24.5 65.1 %reduce-scatter.2.cloned.1.call-done = bf16[8,4096]{1,0:T(8,128)(2,1)} async-done(((bf16[128,4096]{1,0:T(8,128)(2,1)}), bf16[8,4096]{1,0:T(8,128)(2,1)}) %reduce-scatter.2.cloned.1.call-update) | async-done | bytes 65552 | tf_op jit(solution)/shard_map/while/body/eval_jaxpr/reduce_scatter | solution.py:89
  91.2 30.5 %all-gather.2.cloned.1.call-done = bf16[128,4096]{1,0:T(8,128)(2,1)} async-done(((bf16[8,4096]{1,0:T(8,128)(2,1)}), bf16[128,4096]{1,0:T(8,128)(2,1)}) %all-gather.2.cloned.1.call-update) | async-done | bytes 1048592 | tf_op jit(solution)/shard_map/while/body/eval_jaxpr/all_gather | solution.py:122
  123.3 4.4 collective-permute-start
  127.7 2.4 fusion.51
  130.2 83.9 %all-reduce.2.cloned.1.call-done = bf16[1,128,4096]{2,1,0:T(8,128)(2,1)} async-done(((bf16[1,128,4096]{2,1,0:T(8,128)(2,1)}), bf16[1,128,4096]{2,1,0:T(8,128)(2,1)}) %all-reduce.2.cloned.1.call-update) | async-done | bytes 1048592 | tf_op jit(solution)/shard_map/while/body/eval_jaxpr/psum | solution.py:18
  215.0 2.8 fusion.48
  226.4 3.0 convolution_convert_fusion.8
  229.5 60.3 %reduce-scatter.2.cloned.1.call-done = bf16[8,4096]{1,0:T(8,128)(2,1)} async-done(((bf16[128,4096]{1,0:T(8,128)(2,1)}), bf16[8,4096]{1,0:T(8,128)(2,1)}) %reduce-scatter.2.cloned.1.call-update) | async-done | bytes 65552 | tf_op jit(solution)/shard_map/while/body/eval_jaxpr/reduce_scatter | solution.py:89
  291.3 30.7 %all-gather.2.cloned.1.call-done = bf16[128,4096]{1,0:T(8,128)(2,1)} async-done(((bf16[8,4096]{1,0:T(8,128)(2,1)}), bf16[128,4096]{1,0:T(8,128)(2,1)}) %all-gather.2.cloned.1.call-update) | async-done | bytes 1048592 | tf_op jit(solution)/shard_map/while/body/eval_jaxpr/all_gather | solution.py:122
  323.6 4.4 collective-permute-start
  328.0 2.4 fusion.51
  330.5 83.7 %all-reduce.2.cloned.1.call-done = bf16[1,128,4096]{2,1,0:T(8,128)(2,1)} async-done(((bf16[1,128,4096]{2,1,0:T(8,128)(2,1)}), bf16[1,128,4096]{2,1,0:T(8,128)(2,1)}) %all-reduce.2.cloned.1.call-update) | async-done | bytes 1048592 | tf_op jit(solution)/shard_map/while/body/eval_jaxpr/psum | solution.py:18
  415.2 2.8 fusion.48
  426.5 3.0 convolution_convert_fusion.8
  429.7 60.4 %reduce-scatter.2.cloned.1.call-done = bf16[8,4096]{1,0:T(8,128)(2,1)} async-done(((bf16[128,4096]{1,0:T(8,128)(2,1)}), bf16[8,4096]{1,0:T(8,128)(2,1)}) %reduce-scatter.2.cloned.1.call-update) | async-done | bytes 65552 | tf_op jit(solution)/shard_map/while/body/eval_jaxpr/reduce_scatter | solution.py:89
  491.6 30.7 %all-gather.2.cloned.1.call-done = bf16[128,4096]{1,0:T(8,128)(2,1)} async-done(((bf16[8,4096]{1,0:T(8,128)(2,1)}), bf16[128,4096]{1,0:T(8,128)(2,1)}) %all-gather.2.cloned.1.call-update) | async-done | bytes 1048592 | tf_op jit(solution)/shard_map/while/body/eval_jaxpr/all_gather | solution.py:122
  524.0 4.4 collective-permute-start
  528.4 2.4 fusion.51
  530.8 83.8 %all-reduce.2.cloned.1.call-done = bf16[1,128,4096]{2,1,0:T(8,128)(2,1)} async-done(((bf16[1,128,4096]{2,1,0:T(8,128)(2,1)}), bf16[1,128,4096]{2,1,0:T(8,128)(2,1)}) %all-reduce.2.cloned.1.call-update) | async-done | bytes 1048592 | tf_op jit(solution)/shard_map/while/body/eval_jaxpr/psum | solution.py:18
  616.8 2.8 fusion.48
  628.2 3.0 convolution_convert_fusion.8
  631.3 60.4 %reduce-scatter.2.cloned.1.call-done = bf16[8,4096]{1,0:T(8,128)(2,1)} async-done(((bf16[128,4096]{1,0:T(8,128)(2,1)}), bf16[8,4096]{1,0:T(8,128)(2,1)}) %reduce-scatter.2.cloned.1.call-update) | async-done | bytes 65552 | tf_op jit(solution)/shard_map/while/body/eval_jaxpr/reduce_scatter | solution.py:89
  693.3 30.8 %all-gather.2.cloned.1.call-done = bf16[128,4096]{1,0:T(8,128)(2,1)} async-done(((bf16[8,4096]{1,0:T(8,128)(2,1)}), bf16[128,4096]{1,0:T(8,128)(2,1)}) %all-gather.2.cloned.1.call-update) | async-done | bytes 1048592 | tf_op jit(solution)/shard_map/while/body/eval_jaxpr/all_gather | solution.py:122
  725.7 4.4 collective-permute-start
  730.1 2.4 fusion.51
  732.5 83.7 %all-reduce.2.cloned.1.call-done = bf16[1,128,4096]{2,1,0:T(8,128)(2,1)} async-done(((bf16[1,128,4096]{2,1,0:T(8,128)(2,1)}), bf16[1,128,4096]{2,1,0:T(8,128)(2,1)}) %all-reduce.2.cloned.1.call-update) | async-done | bytes 1048592 | tf_op jit(solution)/shard_map/while/body/eval_jaxpr/psum | solution.py:18
  818.5 2.8 fusion.48
  829.8 3.0 convolution_convert_fusion.8
  832.9 60.4 %reduce-scatter.2.cloned.1.call-done = bf16[8,4096]{1,0:T(8,128)(2,1)} async-done(((bf16[128,4096]{1,0:T(8,128)(2,1)}), bf16[8,4096]{1,0:T(8,128)(2,1)}) %reduce-scatter.2.cloned.1.call-update) | async-done | bytes 65552 | tf_op jit(solution)/shard_map/while/body/eval_jaxpr/reduce_scatter | solution.py:89
  894.9 30.5 %all-gather.2.cloned.1.call-done = bf16[128,4096]{1,0:T(8,128)(2,1)} async-done(((bf16[8,4096]{1,0:T(8,128)(2,1)}), bf16[128,4096]{1,0:T(8,128)(2,1)}) %all-gather.2.cloned.1.call-update) | async-done | bytes 1048592 | tf_op jit(solution)/shard_map/while/body/eval_jaxpr/all_gather | solution.py:122
  927.0 4.4 collective-permute-start
  931.5 2.4 fusion.51
  933.9 83.7 %all-reduce.2.cloned.1.call-done = bf16[1,128,4096]{2,1,0:T(8,128)(2,1)} async-done(((bf16[1,128,4096]{2,1,0:T(8,128)(2,1)}), bf16[1,128,4096]{2,1,0:T(8,128)(2,1)}) %all-reduce.2.cloned.1.call-update) | async-done | bytes 1048592 | tf_op jit(solution)/shard_map/while/body/eval_jaxpr/psum | solution.py:18
  1018.6 2.8 fusion.48
  1029.9 3.0 convolution_convert_fusion.8
  1033.0 60.4 %reduce-scatter.2.cloned.1.call-done = bf16[8,4096]{1,0:T(8,128)(2,1)} async-done(((bf16[128,4096]{1,0:T(8,128)(2,1)}), bf16[8,4096]{1,0:T(8,128)(2,1)}) %reduce-scatter.2.cloned.1.call-update) | async-done | bytes 65552 | tf_op jit(solution)/shard_map/while/body/eval_jaxpr/reduce_scatter | solution.py:89
  1095.0 30.7 %all-gather.2.cloned.1.call-done = bf16[128,4096]{1,0:T(8,128)(2,1)} async-done(((bf16[8,4096]{1,0:T(8,128)(2,1)}), bf16[128,4096]{1,0:T(8,128)(2,1)}) %all-gather.2.cloned.1.call-update) | async-done | bytes 1048592 | tf_op jit(solution)/shard_map/while/body/eval_jaxpr/all_gather | solution.py:122
  1127.3 4.4 collective-permute-start
  1131.7 2.4 fusion.51
  1134.1 83.7 %all-reduce.2.cloned.1.call-done = bf16[1,128,4096]{2,1,0:T(8,128)(2,1)} async-done(((bf16[1,128,4096]{2,1,0:T(8,128)(2,1)}), bf16[1,128,4096]{2,1,0:T(8,128)(2,1)}) %all-reduce.2.cloned.1.call-update) | async-done | bytes 1048592 | tf_op jit(solution)/shard_map/while/body/eval_jaxpr/psum | solution.py:18
  1218.9 2.8 fusion.48
  1230.2 3.0 convolution_convert_fusion.8
  1233.3 60.4 %reduce-scatter.2.cloned.1.call-done = bf16[8,4096]{1,0:T(8,128)(2,1)} async-done(((bf16[128,4096]{1,0:T(8,128)(2,1)}), bf16[8,4096]{1,0:T(8,128)(2,1)}) %reduce-scatter.2.cloned.1.call-update) | async-done | bytes 65552 | tf_op jit(solution)/shard_map/while/body/eval_jaxpr/reduce_scatter | solution.py:89
  1295.3 30.7 %all-gather.2.cloned.1.call-done = bf16[128,4096]{1,0:T(8,128)(2,1)} async-done(((bf16[8,4096]{1,0:T(8,128)(2,1)}), bf16[128,4096]{1,0:T(8,128)(2,1)}) %all-gather.2.cloned.1.call-update) | async-done | bytes 1048592 | tf_op jit(solution)/shard_map/while/body/eval_jaxpr/all_gather | solution.py:122
  1327.6 4.4 collective-permute-start
  1332.0 2.4 fusion.51
  1334.4 83.8 %all-reduce.2.cloned.1.call-done = bf16[1,128,4096]{2,1,0:T(8,128)(2,1)} async-done(((bf16[1,128,4096]{2,1,0:T(8,128)(2,1)}), bf16[1,128,4096]{2,1,0:T(8,128)(2,1)}) %all-reduce.2.cloned.1.call-update) | async-done | bytes 1048592 | tf_op jit(solution)/shard_map/while/body/eval_jaxpr/psum | solution.py:18
  1419.2 2.8 fusion.48
  1430.5 3.0 convolution_convert_fusion.8
  1433.7 60.3 %reduce-scatter.2.cloned.1.call-done = bf16[8,4096]{1,0:T(8,128)(2,1)} async-done(((bf16[128,4096]{1,0:T(8,128)(2,1)}), bf16[8,4096]{1,0:T(8,128)(2,1)}) %reduce-scatter.2.cloned.1.call-update) | async-done | bytes 65552 | tf_op jit(solution)/shard_map/while/body/eval_jaxpr/reduce_scatter | solution.py:89
  1495.5 30.9 %all-gather.2.cloned.1.call-done = bf16[128,4096]{1,0:T(8,128)(2,1)} async-done(((bf16[8,4096]{1,0:T(8,128)(2,1)}), bf16[128,4096]{1,0:T(8,128)(2,1)}) %all-gather.2.cloned.1.call-update) | async-done | bytes 1048592 | tf_op jit(solution)/shard_map/while/body/eval_jaxpr/all_gather | solution.py:122
  1528.0 4.4 collective-permute-start
  1532.4 2.4 fusion.51
  1534.8 83.7 %all-reduce.2.cloned.1.call-done = bf16[1,128,4096]{2,1,0:T(8,128)(2,1)} async-done(((bf16[1,128,4096]{2,1,0:T(8,128)(2,1)}), bf16[1,128,4096]{2,1,0:T(8,128)(2,1)}) %all-reduce.2.cloned.1.call-update) | async-done | bytes 1048592 | tf_op jit(solution)/shard_map/while/body/eval_jaxpr/psum | solution.py:18
  1619.6 2.8 fusion.48
  1630.9 3.0 convolution_convert_fusion.8
  1634.0 60.4 %reduce-scatter.2.cloned.1.call-done = bf16[8,4096]{1,0:T(8,128)(2,1)} async-done(((bf16[128,4096]{1,0:T(8,128)(2,1)}), bf16[8,4096]{1,0:T(8,128)(2,1)}) %reduce-scatter.2.cloned.1.call-update) | async-done | bytes 65552 | tf_op jit(solution)/shard_map/while/body/eval_jaxpr/reduce_scatter | solution.py:89
  1696.0 30.6 %all-gather.2.cloned.1.call-done = bf16[128,4096]{1,0:T(8,128)(2,1)} async-done(((bf16[8,4096]{1,0:T(8,128)(2,1)}), bf16[128,4096]{1,0:T(8,128)(2,1)}) %all-gather.2.cloned.1.call-update) | async-done | bytes 1048592 | tf_op jit(solution)/shard_map/while/body/eval_jaxpr/all_gather | solution.py:122
  1728.2 4.4 collective-permute-start
  1732.6 2.4 fusion.51
  1735.1 83.7 %all-reduce.2.cloned.1.call-done = bf16[1,128,4096]{2,1,0:T(8,128)(2,1)} async-done(((bf16[1,128,4096]{2,1,0:T(8,128)(2,1)}), bf16[1,128,4096]{2,1,0:T(8,128)(2,1)}) %all-reduce.2.cloned.1.call-update) | async-done | bytes 1048592 | tf_op jit(solution)/shard_map/while/body/eval_jaxpr/psum | solution.py:18
  (315 shorter events, 118.3 us)
Async XLA Ops:
  7.6 1.8 copy-start.7
  9.5 80.2 %reduce-scatter.2.cloned.1.call-start = ((), (), s32[]{:S(2)}) async-start(), calls=%async_computation.1 | async-start | bytes 1114112 | tf_op jit(solution)/shard_map/while/body/eval_jaxpr/reduce_scatter | solution.py:89
  10.1 2.9 copy-start.6
  24.5 97.2 %all-gather.2.cloned.1.call-start = ((), (), s32[]{:S(2)}) async-start(), calls=%async_computation.2 | async-start | bytes 1114112 | tf_op jit(solution)/shard_map/while/body/eval_jaxpr/all_gather | solution.py:122
  91.1 122.9 %all-reduce.2.cloned.1.call-start = ((), (), s32[]{:S(2)}) async-start(), calls=%async_computation.3 | async-start | bytes 2097152 | tf_op jit(solution)/shard_map/while/body/eval_jaxpr/psum | solution.py:18
  123.3 91.1 %collective-permute-start = (bf16[128,4096]{1,0:T(8,128)(2,1)S(1)}, bf16[128,4096]{1,0:T(8,128)(2,1)}, u32[]{:S(2)}, u32[]{:S(2)}) collective-permute-start(bf16[128,4096]{1,0:T(8,128)(2,1)S(1)} %copy-done), channel_id=1, source_target_pairs={{0,16},{16,32},{32,48},{48,64},{64,80},{80,96},{96,112},{1,17},{17... | collective-permute-start | bytes 3145736 | tf_op jit(solution)/shard_map/while/body/eval_jaxpr/ppermute | solution.py:13
  130.2 84.2 %copy-start.5 = (f32[4096]{0:T(1024)S(1)}, f32[4096]{0:T(1024)}, u32[]{:S(2)}) copy-start(f32[4096]{0:T(1024)} %get-tuple-element.671) | copy-start | bytes 49156 | tf_op jit(solution)/shard_map/while
  130.2 84.2 %copy-start.8 = (f32[1,4]{1,0:T(1,128)S(1)}, f32[1,4]{1,0:T(1,128)}, u32[]{:S(2)}) copy-start(f32[1,4]{1,0:T(1,128)} %get-tuple-element.697) | copy-start | bytes 52 | tf_op jit(solution)/shard_map/while
  214.4 75.3 %reduce-scatter.2.cloned.1.call-start = ((), (), s32[]{:S(2)}) async-start(), calls=%async_computation.1 | async-start | bytes 1114112 | tf_op jit(solution)/shard_map/while/body/eval_jaxpr/reduce_scatter | solution.py:89
  215.0 2.9 copy-start.6
  229.4 92.6 %all-gather.2.cloned.1.call-start = ((), (), s32[]{:S(2)}) async-start(), calls=%async_computation.2 | async-start | bytes 1114112 | tf_op jit(solution)/shard_map/while/body/eval_jaxpr/all_gather | solution.py:122
  291.3 122.9 %all-reduce.2.cloned.1.call-start = ((), (), s32[]{:S(2)}) async-start(), calls=%async_computation.3 | async-start | bytes 2097152 | tf_op jit(solution)/shard_map/while/body/eval_jaxpr/psum | solution.py:18
  323.6 90.9 %collective-permute-start = (bf16[128,4096]{1,0:T(8,128)(2,1)S(1)}, bf16[128,4096]{1,0:T(8,128)(2,1)}, u32[]{:S(2)}, u32[]{:S(2)}) collective-permute-start(bf16[128,4096]{1,0:T(8,128)(2,1)S(1)} %copy-done), channel_id=1, source_target_pairs={{0,16},{16,32},{32,48},{48,64},{64,80},{80,96},{96,112},{1,17},{17... | collective-permute-start | bytes 3145736 | tf_op jit(solution)/shard_map/while/body/eval_jaxpr/ppermute | solution.py:13
  330.5 84.1 %copy-start.5 = (f32[4096]{0:T(1024)S(1)}, f32[4096]{0:T(1024)}, u32[]{:S(2)}) copy-start(f32[4096]{0:T(1024)} %get-tuple-element.671) | copy-start | bytes 49156 | tf_op jit(solution)/shard_map/while
  330.5 84.1 %copy-start.8 = (f32[1,4]{1,0:T(1,128)S(1)}, f32[1,4]{1,0:T(1,128)}, u32[]{:S(2)}) copy-start(f32[1,4]{1,0:T(1,128)} %get-tuple-element.697) | copy-start | bytes 52 | tf_op jit(solution)/shard_map/while
  414.6 75.5 %reduce-scatter.2.cloned.1.call-start = ((), (), s32[]{:S(2)}) async-start(), calls=%async_computation.1 | async-start | bytes 1114112 | tf_op jit(solution)/shard_map/while/body/eval_jaxpr/reduce_scatter | solution.py:89
  415.2 2.9 copy-start.6
  429.6 92.7 %all-gather.2.cloned.1.call-start = ((), (), s32[]{:S(2)}) async-start(), calls=%async_computation.2 | async-start | bytes 1114112 | tf_op jit(solution)/shard_map/while/body/eval_jaxpr/all_gather | solution.py:122
  491.6 123.1 %all-reduce.2.cloned.1.call-start = ((), (), s32[]{:S(2)}) async-start(), calls=%async_computation.3 | async-start | bytes 2097152 | tf_op jit(solution)/shard_map/while/body/eval_jaxpr/psum | solution.py:18
  524.0 92.2 %collective-permute-start = (bf16[128,4096]{1,0:T(8,128)(2,1)S(1)}, bf16[128,4096]{1,0:T(8,128)(2,1)}, u32[]{:S(2)}, u32[]{:S(2)}) collective-permute-start(bf16[128,4096]{1,0:T(8,128)(2,1)S(1)} %copy-done), channel_id=1, source_target_pairs={{0,16},{16,32},{32,48},{48,64},{64,80},{80,96},{96,112},{1,17},{17... | collective-permute-start | bytes 3145736 | tf_op jit(solution)/shard_map/while/body/eval_jaxpr/ppermute | solution.py:13
  530.8 85.4 %copy-start.5 = (f32[4096]{0:T(1024)S(1)}, f32[4096]{0:T(1024)}, u32[]{:S(2)}) copy-start(f32[4096]{0:T(1024)} %get-tuple-element.671) | copy-start | bytes 49156 | tf_op jit(solution)/shard_map/while
  530.8 85.4 %copy-start.8 = (f32[1,4]{1,0:T(1,128)S(1)}, f32[1,4]{1,0:T(1,128)}, u32[]{:S(2)}) copy-start(f32[1,4]{1,0:T(1,128)} %get-tuple-element.697) | copy-start | bytes 52 | tf_op jit(solution)/shard_map/while
  616.2 75.5 %reduce-scatter.2.cloned.1.call-start = ((), (), s32[]{:S(2)}) async-start(), calls=%async_computation.1 | async-start | bytes 1114112 | tf_op jit(solution)/shard_map/while/body/eval_jaxpr/reduce_scatter | solution.py:89
  616.8 2.9 copy-start.6
  631.2 92.8 %all-gather.2.cloned.1.call-start = ((), (), s32[]{:S(2)}) async-start(), calls=%async_computation.2 | async-start | bytes 1114112 | tf_op jit(solution)/shard_map/while/body/eval_jaxpr/all_gather | solution.py:122
  693.2 123.0 %all-reduce.2.cloned.1.call-start = ((), (), s32[]{:S(2)}) async-start(), calls=%async_computation.3 | async-start | bytes 2097152 | tf_op jit(solution)/shard_map/while/body/eval_jaxpr/psum | solution.py:18
  725.7 92.2 %collective-permute-start = (bf16[128,4096]{1,0:T(8,128)(2,1)S(1)}, bf16[128,4096]{1,0:T(8,128)(2,1)}, u32[]{:S(2)}, u32[]{:S(2)}) collective-permute-start(bf16[128,4096]{1,0:T(8,128)(2,1)S(1)} %copy-done), channel_id=1, source_target_pairs={{0,16},{16,32},{32,48},{48,64},{64,80},{80,96},{96,112},{1,17},{17... | collective-permute-start | bytes 3145736 | tf_op jit(solution)/shard_map/while/body/eval_jaxpr/ppermute | solution.py:13
  732.5 85.3 %copy-start.5 = (f32[4096]{0:T(1024)S(1)}, f32[4096]{0:T(1024)}, u32[]{:S(2)}) copy-start(f32[4096]{0:T(1024)} %get-tuple-element.671) | copy-start | bytes 49156 | tf_op jit(solution)/shard_map/while
  732.5 85.3 %copy-start.8 = (f32[1,4]{1,0:T(1,128)S(1)}, f32[1,4]{1,0:T(1,128)}, u32[]{:S(2)}) copy-start(f32[1,4]{1,0:T(1,128)} %get-tuple-element.697) | copy-start | bytes 52 | tf_op jit(solution)/shard_map/while
  817.9 75.5 %reduce-scatter.2.cloned.1.call-start = ((), (), s32[]{:S(2)}) async-start(), calls=%async_computation.1 | async-start | bytes 1114112 | tf_op jit(solution)/shard_map/while/body/eval_jaxpr/reduce_scatter | solution.py:89
  818.5 2.9 copy-start.6
  832.9 92.5 %all-gather.2.cloned.1.call-start = ((), (), s32[]{:S(2)}) async-start(), calls=%async_computation.2 | async-start | bytes 1114112 | tf_op jit(solution)/shard_map/while/body/eval_jaxpr/all_gather | solution.py:122
  894.8 122.8 %all-reduce.2.cloned.1.call-start = ((), (), s32[]{:S(2)}) async-start(), calls=%async_computation.3 | async-start | bytes 2097152 | tf_op jit(solution)/shard_map/while/body/eval_jaxpr/psum | solution.py:18
  927.0 90.9 %collective-permute-start = (bf16[128,4096]{1,0:T(8,128)(2,1)S(1)}, bf16[128,4096]{1,0:T(8,128)(2,1)}, u32[]{:S(2)}, u32[]{:S(2)}) collective-permute-start(bf16[128,4096]{1,0:T(8,128)(2,1)S(1)} %copy-done), channel_id=1, source_target_pairs={{0,16},{16,32},{32,48},{48,64},{64,80},{80,96},{96,112},{1,17},{17... | collective-permute-start | bytes 3145736 | tf_op jit(solution)/shard_map/while/body/eval_jaxpr/ppermute | solution.py:13
  933.9 84.1 %copy-start.5 = (f32[4096]{0:T(1024)S(1)}, f32[4096]{0:T(1024)}, u32[]{:S(2)}) copy-start(f32[4096]{0:T(1024)} %get-tuple-element.671) | copy-start | bytes 49156 | tf_op jit(solution)/shard_map/while
  933.9 84.1 %copy-start.8 = (f32[1,4]{1,0:T(1,128)S(1)}, f32[1,4]{1,0:T(1,128)}, u32[]{:S(2)}) copy-start(f32[1,4]{1,0:T(1,128)} %get-tuple-element.697) | copy-start | bytes 52 | tf_op jit(solution)/shard_map/while
  1018.0 75.5 %reduce-scatter.2.cloned.1.call-start = ((), (), s32[]{:S(2)}) async-start(), calls=%async_computation.1 | async-start | bytes 1114112 | tf_op jit(solution)/shard_map/while/body/eval_jaxpr/reduce_scatter | solution.py:89
  1018.6 2.9 copy-start.6
  1033.0 92.7 %all-gather.2.cloned.1.call-start = ((), (), s32[]{:S(2)}) async-start(), calls=%async_computation.2 | async-start | bytes 1114112 | tf_op jit(solution)/shard_map/while/body/eval_jaxpr/all_gather | solution.py:122
  1094.9 122.9 %all-reduce.2.cloned.1.call-start = ((), (), s32[]{:S(2)}) async-start(), calls=%async_computation.3 | async-start | bytes 2097152 | tf_op jit(solution)/shard_map/while/body/eval_jaxpr/psum | solution.py:18
  1127.3 90.9 %collective-permute-start = (bf16[128,4096]{1,0:T(8,128)(2,1)S(1)}, bf16[128,4096]{1,0:T(8,128)(2,1)}, u32[]{:S(2)}, u32[]{:S(2)}) collective-permute-start(bf16[128,4096]{1,0:T(8,128)(2,1)S(1)} %copy-done), channel_id=1, source_target_pairs={{0,16},{16,32},{32,48},{48,64},{64,80},{80,96},{96,112},{1,17},{17... | collective-permute-start | bytes 3145736 | tf_op jit(solution)/shard_map/while/body/eval_jaxpr/ppermute | solution.py:13
  1134.1 84.1 %copy-start.5 = (f32[4096]{0:T(1024)S(1)}, f32[4096]{0:T(1024)}, u32[]{:S(2)}) copy-start(f32[4096]{0:T(1024)} %get-tuple-element.671) | copy-start | bytes 49156 | tf_op jit(solution)/shard_map/while
  1134.1 84.1 %copy-start.8 = (f32[1,4]{1,0:T(1,128)S(1)}, f32[1,4]{1,0:T(1,128)}, u32[]{:S(2)}) copy-start(f32[1,4]{1,0:T(1,128)} %get-tuple-element.697) | copy-start | bytes 52 | tf_op jit(solution)/shard_map/while
  1218.3 75.5 %reduce-scatter.2.cloned.1.call-start = ((), (), s32[]{:S(2)}) async-start(), calls=%async_computation.1 | async-start | bytes 1114112 | tf_op jit(solution)/shard_map/while/body/eval_jaxpr/reduce_scatter | solution.py:89
  1218.9 2.9 copy-start.6
  1233.3 92.7 %all-gather.2.cloned.1.call-start = ((), (), s32[]{:S(2)}) async-start(), calls=%async_computation.2 | async-start | bytes 1114112 | tf_op jit(solution)/shard_map/while/body/eval_jaxpr/all_gather | solution.py:122
  1295.2 123.0 %all-reduce.2.cloned.1.call-start = ((), (), s32[]{:S(2)}) async-start(), calls=%async_computation.3 | async-start | bytes 2097152 | tf_op jit(solution)/shard_map/while/body/eval_jaxpr/psum | solution.py:18
  1327.6 91.0 %collective-permute-start = (bf16[128,4096]{1,0:T(8,128)(2,1)S(1)}, bf16[128,4096]{1,0:T(8,128)(2,1)}, u32[]{:S(2)}, u32[]{:S(2)}) collective-permute-start(bf16[128,4096]{1,0:T(8,128)(2,1)S(1)} %copy-done), channel_id=1, source_target_pairs={{0,16},{16,32},{32,48},{48,64},{64,80},{80,96},{96,112},{1,17},{17... | collective-permute-start | bytes 3145736 | tf_op jit(solution)/shard_map/while/body/eval_jaxpr/ppermute | solution.py:13
  1334.4 84.1 %copy-start.5 = (f32[4096]{0:T(1024)S(1)}, f32[4096]{0:T(1024)}, u32[]{:S(2)}) copy-start(f32[4096]{0:T(1024)} %get-tuple-element.671) | copy-start | bytes 49156 | tf_op jit(solution)/shard_map/while
  1334.4 84.1 %copy-start.8 = (f32[1,4]{1,0:T(1,128)S(1)}, f32[1,4]{1,0:T(1,128)}, u32[]{:S(2)}) copy-start(f32[1,4]{1,0:T(1,128)} %get-tuple-element.697) | copy-start | bytes 52 | tf_op jit(solution)/shard_map/while
  1418.6 75.3 %reduce-scatter.2.cloned.1.call-start = ((), (), s32[]{:S(2)}) async-start(), calls=%async_computation.1 | async-start | bytes 1114112 | tf_op jit(solution)/shard_map/while/body/eval_jaxpr/reduce_scatter | solution.py:89
  1419.2 2.9 copy-start.6
  1433.6 92.8 %all-gather.2.cloned.1.call-start = ((), (), s32[]{:S(2)}) async-start(), calls=%async_computation.2 | async-start | bytes 1114112 | tf_op jit(solution)/shard_map/while/body/eval_jaxpr/all_gather | solution.py:122
  1495.4 123.2 %all-reduce.2.cloned.1.call-start = ((), (), s32[]{:S(2)}) async-start(), calls=%async_computation.3 | async-start | bytes 2097152 | tf_op jit(solution)/shard_map/while/body/eval_jaxpr/psum | solution.py:18
  1528.0 90.9 %collective-permute-start = (bf16[128,4096]{1,0:T(8,128)(2,1)S(1)}, bf16[128,4096]{1,0:T(8,128)(2,1)}, u32[]{:S(2)}, u32[]{:S(2)}) collective-permute-start(bf16[128,4096]{1,0:T(8,128)(2,1)S(1)} %copy-done), channel_id=1, source_target_pairs={{0,16},{16,32},{32,48},{48,64},{64,80},{80,96},{96,112},{1,17},{17... | collective-permute-start | bytes 3145736 | tf_op jit(solution)/shard_map/while/body/eval_jaxpr/ppermute | solution.py:13
  1534.8 84.1 %copy-start.5 = (f32[4096]{0:T(1024)S(1)}, f32[4096]{0:T(1024)}, u32[]{:S(2)}) copy-start(f32[4096]{0:T(1024)} %get-tuple-element.671) | copy-start | bytes 49156 | tf_op jit(solution)/shard_map/while
  1534.8 84.1 %copy-start.8 = (f32[1,4]{1,0:T(1,128)S(1)}, f32[1,4]{1,0:T(1,128)}, u32[]{:S(2)}) copy-start(f32[1,4]{1,0:T(1,128)} %get-tuple-element.697) | copy-start | bytes 52 | tf_op jit(solution)/shard_map/while
  1619.0 75.5 %reduce-scatter.2.cloned.1.call-start = ((), (), s32[]{:S(2)}) async-start(), calls=%async_computation.1 | async-start | bytes 1114112 | tf_op jit(solution)/shard_map/while/body/eval_jaxpr/reduce_scatter | solution.py:89
  1619.6 2.9 copy-start.6
  1634.0 92.6 %all-gather.2.cloned.1.call-start = ((), (), s32[]{:S(2)}) async-start(), calls=%async_computation.2 | async-start | bytes 1114112 | tf_op jit(solution)/shard_map/while/body/eval_jaxpr/all_gather | solution.py:122
  1696.0 122.8 %all-reduce.2.cloned.1.call-start = ((), (), s32[]{:S(2)}) async-start(), calls=%async_computation.3 | async-start | bytes 2097152 | tf_op jit(solution)/shard_map/while/body/eval_jaxpr/psum | solution.py:18
  1728.2 90.9 %collective-permute-start = (bf16[128,4096]{1,0:T(8,128)(2,1)S(1)}, bf16[128,4096]{1,0:T(8,128)(2,1)}, u32[]{:S(2)}, u32[]{:S(2)}) collective-permute-start(bf16[128,4096]{1,0:T(8,128)(2,1)S(1)} %copy-done), channel_id=1, source_target_pairs={{0,16},{16,32},{32,48},{48,64},{64,80},{80,96},{96,112},{1,17},{17... | collective-permute-start | bytes 3145736 | tf_op jit(solution)/shard_map/while/body/eval_jaxpr/ppermute | solution.py:13
  1735.1 84.1 %copy-start.5 = (f32[4096]{0:T(1024)S(1)}, f32[4096]{0:T(1024)}, u32[]{:S(2)}) copy-start(f32[4096]{0:T(1024)} %get-tuple-element.671) | copy-start | bytes 49156 | tf_op jit(solution)/shard_map/while
  1735.1 84.1 %copy-start.8 = (f32[1,4]{1,0:T(1,128)S(1)}, f32[1,4]{1,0:T(1,128)}, u32[]{:S(2)}) copy-start(f32[1,4]{1,0:T(1,128)} %get-tuple-element.697) | copy-start | bytes 52 | tf_op jit(solution)/shard_map/while
  (29 other events, 47.6 us)
Sparse Core Ops, SparseCore 0:
  24.6 65.0 reduce-scatter.1
  91.3 30.3 all-gather.1
  124.2 89.7 all-reduce.1
  229.6 60.1 reduce-scatter.1
  291.4 30.5 all-gather.1
  324.3 89.8 all-reduce.1
  429.7 60.2 reduce-scatter.1
  491.8 30.5 all-gather.1
  524.9 89.7 all-reduce.1
  631.3 60.3 reduce-scatter.1
  693.4 30.5 all-gather.1
  726.4 89.8 all-reduce.1
  833.0 60.2 reduce-scatter.1
  895.0 30.4 all-gather.1
  927.8 89.7 all-reduce.1
  1033.1 60.2 reduce-scatter.1
  1095.1 30.5 all-gather.1
  1128.0 89.8 all-reduce.1
  1233.4 60.2 reduce-scatter.1
  1295.4 30.5 all-gather.1
  1328.5 89.7 all-reduce.1
  1433.7 60.1 reduce-scatter.1
  1495.6 30.6 all-gather.1
  1528.7 89.8 all-reduce.1
  1634.1 60.3 reduce-scatter.1
  1696.1 30.4 all-gather.1
  1728.9 89.7 all-reduce.1
where the time goes:
time: 1830 us
  waiting for transfers between devices  1580 us (86%)
  other arithmetic  91.7 us (5%)
  matrix products  74.8 us (4%)
  starting transfers between devices  41 us (2%)
  local copies, waits for them, and re-layouts  25.1 us (1%)
    psum x9, waiting for transfers between devices, broadcast(): return lax.psum(kept, axis)  754 us
    reduce_scatter x9, waiting for transfers between devices, layer(): lax.psum_scatter(jnp.dot(blended_payloads, w_output, preferred_element_ty...  548 us
    all_gather x9, waiting for transfers between devices, advance(): outgoing = lax.all_gather(share, 'seq', axis=0, tiled=True)  276 us
    ppermute x9, starting transfers between devices, from_behind(): return lax.ppermute(x, axis, pairs)  39.8 us
  transfers between devices with their start and end apart: 36, of which 27 were waited for; matrix products, arithmetic and copies ran while one was open for 1% of the time, Pallas kernels for 0%

commit v1 on v0

--- a/solution.py
+++ b/solution.py
@@ -119,7 +119,8 @@
             jnp.where(present_layer_index == encoders, target_rows, arrived_rows),
         )
         share = layer(stream, memory_kept)
-        outgoing = lax.all_gather(share, "seq", axis=0, tiled=True)
+        sent = jnp.stack([share] * lax.axis_size("seq"))
+        outgoing = jnp.concatenate(lax.all_to_all(sent, "seq", 0, 0), axis=0)
         written = lax.dynamic_update_index_in_dim(finished, outgoing, batch_index, 0)
         finished = jnp.where(valid, written, finished)
         arrived = from_behind(outgoing, "section", 1)

time: 1830 us -> 1720 us (0.940)
  waiting for transfers between devices: 1580 us -> 1440 us
  starting transfers between devices: 41 us -> 74.2 us
    all_gather x9 -> x0, waiting for transfers between devices: 276 us -> none  [advance(): outgoing = lax.all_gather(share, 'seq', axis=0, tiled=True)]
    all_to_all x0 -> x9, waiting for transfers between devices: none -> 147 us  [advance(): outgoing = jnp.concatenate(lax.all_to_all(sent, 'seq', 0, 0), axis=0)]
    all_to_all x0 -> x9, starting transfers between devices: none -> 32.9 us  [advance(): outgoing = jnp.concatenate(lax.all_to_all(sent, 'seq', 0, 0), axis=0)]
  transfers between devices with their start and end apart: 36 -> 36, of which waited for: 27 -> 27; matrix products, arithmetic and copies ran while one was open for 1% -> 2% of each run, Pallas kernels for 0% -> 0%
where the time goes in v1:
time: 1720 us
  waiting for transfers between devices  1440 us (84%)
  other arithmetic  85.6 us (5%)
  matrix products  75 us (4%)
  starting transfers between devices  74.2 us (4%)
  local copies, waits for them, and re-layouts  30.6 us (2%)
    psum x9, waiting for transfers between devices, broadcast(): return lax.psum(kept, axis)  740 us
    reduce_scatter x9, waiting for transfers between devices, layer(): lax.psum_scatter(jnp.dot(blended_payloads, w_output, preferred_element_ty...  549 us
    all_to_all x9, waiting for transfers between devices, advance(): outgoing = jnp.concatenate(lax.all_to_all(sent, 'seq', 0, 0), axis=0)  147 us
    ppermute x9, starting transfers between devices, from_behind(): return lax.ppermute(x, axis, pairs)  40.6 us
  transfers between devices with their start and end apart: 36, of which 27 were waited for; matrix products, arithmetic and copies ran while one was open for 2% of the time, Pallas kernels for 0%

profile of v1, /device:TPU:0, one launch (start us, length us, event | category | flops | bytes accessed | tf_op | source)
XLA Modules:
  0.0 1716.1 jit_solution(12866470893001033991)
XLA Ops:
  9.5 1699.7 %while.19 = (s32[]{:T(128)}, bf16[128,4096]{1,0:T(8,128)(2,1)}, bf16[2,128,4096]{2,1,0:T(8,128)(2,1)S(1)}, bf16[2,128,4096]{2,1,0:T(8,128)(2,1)}, pred[]{:T(512)...) while((s32[]{:T(128)}, bf16[128,4096]{1,0:T(8,128)(2,1)}, ...), condition=%wide.region_8.9_spmd, body=%wide.region_0.8_spmd.sunk | while | flops 1104807808 | bytes 74388784 | solution.py:136
  10.0 2.8 fusion.48
  21.4 3.1 convolution_convert_fusion.8
  24.4 65.2 %reduce-scatter.2.cloned.1.call-done = bf16[8,4096]{1,0:T(8,128)(2,1)} async-done(((bf16[128,4096]{1,0:T(8,128)(2,1)}), bf16[8,4096]{1,0:T(8,128)(2,1)}) %reduce-scatter.2.cloned.1.call-update) | async-done | bytes 65552 | tf_op jit(solution)/shard_map/while/body/eval_jaxpr/reduce_scatter | solution.py:89
  91.6 3.7 all-to-all-start
  95.3 16.4 all-to-all-done
  112.8 4.4 collective-permute-start
  119.6 82.0 %all-reduce.2.cloned.1.call-done = bf16[1,128,4096]{2,1,0:T(8,128)(2,1)} async-done(((bf16[1,128,4096]{2,1,0:T(8,128)(2,1)}), bf16[1,128,4096]{2,1,0:T(8,128)(2,1)}) %all-reduce.2.cloned.1.call-update) | async-done | bytes 1048592 | tf_op jit(solution)/shard_map/while/body/eval_jaxpr/psum | solution.py:18
  202.5 2.8 fusion.48
  213.8 3.1 convolution_convert_fusion.8
  216.9 60.5 %reduce-scatter.2.cloned.1.call-done = bf16[8,4096]{1,0:T(8,128)(2,1)} async-done(((bf16[128,4096]{1,0:T(8,128)(2,1)}), bf16[8,4096]{1,0:T(8,128)(2,1)}) %reduce-scatter.2.cloned.1.call-update) | async-done | bytes 65552 | tf_op jit(solution)/shard_map/while/body/eval_jaxpr/reduce_scatter | solution.py:89
  279.4 3.7 all-to-all-start
  283.1 16.4 all-to-all-done
  300.6 4.3 collective-permute-start
  307.3 82.4 %all-reduce.2.cloned.1.call-done = bf16[1,128,4096]{2,1,0:T(8,128)(2,1)} async-done(((bf16[1,128,4096]{2,1,0:T(8,128)(2,1)}), bf16[1,128,4096]{2,1,0:T(8,128)(2,1)}) %all-reduce.2.cloned.1.call-update) | async-done | bytes 1048592 | tf_op jit(solution)/shard_map/while/body/eval_jaxpr/psum | solution.py:18
  390.7 2.8 fusion.48
  402.0 3.1 convolution_convert_fusion.8
  405.1 60.4 %reduce-scatter.2.cloned.1.call-done = bf16[8,4096]{1,0:T(8,128)(2,1)} async-done(((bf16[128,4096]{1,0:T(8,128)(2,1)}), bf16[8,4096]{1,0:T(8,128)(2,1)}) %reduce-scatter.2.cloned.1.call-update) | async-done | bytes 65552 | tf_op jit(solution)/shard_map/while/body/eval_jaxpr/reduce_scatter | solution.py:89
  467.4 3.7 all-to-all-start
  471.1 16.4 all-to-all-done
  488.6 4.6 collective-permute-start
  495.7 82.2 %all-reduce.2.cloned.1.call-done = bf16[1,128,4096]{2,1,0:T(8,128)(2,1)} async-done(((bf16[1,128,4096]{2,1,0:T(8,128)(2,1)}), bf16[1,128,4096]{2,1,0:T(8,128)(2,1)}) %all-reduce.2.cloned.1.call-update) | async-done | bytes 1048592 | tf_op jit(solution)/shard_map/while/body/eval_jaxpr/psum | solution.py:18
  580.0 2.8 fusion.48
  591.4 3.1 convolution_convert_fusion.8
  594.4 60.4 %reduce-scatter.2.cloned.1.call-done = bf16[8,4096]{1,0:T(8,128)(2,1)} async-done(((bf16[128,4096]{1,0:T(8,128)(2,1)}), bf16[8,4096]{1,0:T(8,128)(2,1)}) %reduce-scatter.2.cloned.1.call-update) | async-done | bytes 65552 | tf_op jit(solution)/shard_map/while/body/eval_jaxpr/reduce_scatter | solution.py:89
  656.8 3.7 all-to-all-start
  660.5 16.4 all-to-all-done
  678.0 4.6 collective-permute-start
  685.0 82.0 %all-reduce.2.cloned.1.call-done = bf16[1,128,4096]{2,1,0:T(8,128)(2,1)} async-done(((bf16[1,128,4096]{2,1,0:T(8,128)(2,1)}), bf16[1,128,4096]{2,1,0:T(8,128)(2,1)}) %all-reduce.2.cloned.1.call-update) | async-done | bytes 1048592 | tf_op jit(solution)/shard_map/while/body/eval_jaxpr/psum | solution.py:18
  769.2 2.8 fusion.48
  780.6 3.1 convolution_convert_fusion.8
  783.6 60.4 %reduce-scatter.2.cloned.1.call-done = bf16[8,4096]{1,0:T(8,128)(2,1)} async-done(((bf16[128,4096]{1,0:T(8,128)(2,1)}), bf16[8,4096]{1,0:T(8,128)(2,1)}) %reduce-scatter.2.cloned.1.call-update) | async-done | bytes 65552 | tf_op jit(solution)/shard_map/while/body/eval_jaxpr/reduce_scatter | solution.py:89
  846.0 3.7 all-to-all-start
  849.7 16.4 all-to-all-done
  867.2 4.6 collective-permute-start
  874.3 82.0 %all-reduce.2.cloned.1.call-done = bf16[1,128,4096]{2,1,0:T(8,128)(2,1)} async-done(((bf16[1,128,4096]{2,1,0:T(8,128)(2,1)}), bf16[1,128,4096]{2,1,0:T(8,128)(2,1)}) %all-reduce.2.cloned.1.call-update) | async-done | bytes 1048592 | tf_op jit(solution)/shard_map/while/body/eval_jaxpr/psum | solution.py:18
  957.2 2.8 fusion.48
  968.6 3.1 convolution_convert_fusion.8
  971.6 60.4 %reduce-scatter.2.cloned.1.call-done = bf16[8,4096]{1,0:T(8,128)(2,1)} async-done(((bf16[128,4096]{1,0:T(8,128)(2,1)}), bf16[8,4096]{1,0:T(8,128)(2,1)}) %reduce-scatter.2.cloned.1.call-update) | async-done | bytes 65552 | tf_op jit(solution)/shard_map/while/body/eval_jaxpr/reduce_scatter | solution.py:89
  1033.9 3.7 all-to-all-start
  1037.7 16.4 all-to-all-done
  1055.2 4.6 collective-permute-start
  1062.2 82.2 %all-reduce.2.cloned.1.call-done = bf16[1,128,4096]{2,1,0:T(8,128)(2,1)} async-done(((bf16[1,128,4096]{2,1,0:T(8,128)(2,1)}), bf16[1,128,4096]{2,1,0:T(8,128)(2,1)}) %all-reduce.2.cloned.1.call-update) | async-done | bytes 1048592 | tf_op jit(solution)/shard_map/while/body/eval_jaxpr/psum | solution.py:18
  1145.4 2.8 fusion.48
  1156.7 3.1 convolution_convert_fusion.8
  1159.8 60.4 %reduce-scatter.2.cloned.1.call-done = bf16[8,4096]{1,0:T(8,128)(2,1)} async-done(((bf16[128,4096]{1,0:T(8,128)(2,1)}), bf16[8,4096]{1,0:T(8,128)(2,1)}) %reduce-scatter.2.cloned.1.call-update) | async-done | bytes 65552 | tf_op jit(solution)/shard_map/while/body/eval_jaxpr/reduce_scatter | solution.py:89
  1222.1 3.7 all-to-all-start
  1225.8 16.4 all-to-all-done
  1243.4 4.6 collective-permute-start
  1250.4 82.2 %all-reduce.2.cloned.1.call-done = bf16[1,128,4096]{2,1,0:T(8,128)(2,1)} async-done(((bf16[1,128,4096]{2,1,0:T(8,128)(2,1)}), bf16[1,128,4096]{2,1,0:T(8,128)(2,1)}) %all-reduce.2.cloned.1.call-update) | async-done | bytes 1048592 | tf_op jit(solution)/shard_map/while/body/eval_jaxpr/psum | solution.py:18
  1333.5 2.8 fusion.48
  1344.8 3.1 convolution_convert_fusion.8
  1347.9 60.4 %reduce-scatter.2.cloned.1.call-done = bf16[8,4096]{1,0:T(8,128)(2,1)} async-done(((bf16[128,4096]{1,0:T(8,128)(2,1)}), bf16[8,4096]{1,0:T(8,128)(2,1)}) %reduce-scatter.2.cloned.1.call-update) | async-done | bytes 65552 | tf_op jit(solution)/shard_map/while/body/eval_jaxpr/reduce_scatter | solution.py:89
  1410.3 3.7 all-to-all-start
  1414.0 16.4 all-to-all-done
  1431.5 4.4 collective-permute-start
  1438.4 82.2 %all-reduce.2.cloned.1.call-done = bf16[1,128,4096]{2,1,0:T(8,128)(2,1)} async-done(((bf16[1,128,4096]{2,1,0:T(8,128)(2,1)}), bf16[1,128,4096]{2,1,0:T(8,128)(2,1)}) %all-reduce.2.cloned.1.call-update) | async-done | bytes 1048592 | tf_op jit(solution)/shard_map/while/body/eval_jaxpr/psum | solution.py:18
  1521.6 2.8 fusion.48
  1532.9 3.1 convolution_convert_fusion.8
  1536.0 60.4 %reduce-scatter.2.cloned.1.call-done = bf16[8,4096]{1,0:T(8,128)(2,1)} async-done(((bf16[128,4096]{1,0:T(8,128)(2,1)}), bf16[8,4096]{1,0:T(8,128)(2,1)}) %reduce-scatter.2.cloned.1.call-update) | async-done | bytes 65552 | tf_op jit(solution)/shard_map/while/body/eval_jaxpr/reduce_scatter | solution.py:89
  1598.4 3.7 all-to-all-start
  1602.1 16.4 all-to-all-done
  1619.6 4.6 collective-permute-start
  1626.6 82.2 %all-reduce.2.cloned.1.call-done = bf16[1,128,4096]{2,1,0:T(8,128)(2,1)} async-done(((bf16[1,128,4096]{2,1,0:T(8,128)(2,1)}), bf16[1,128,4096]{2,1,0:T(8,128)(2,1)}) %all-reduce.2.cloned.1.call-update) | async-done | bytes 1048592 | tf_op jit(solution)/shard_map/while/body/eval_jaxpr/psum | solution.py:18
  (297 shorter events, 139.3 us)
Async XLA Ops:
  7.6 1.8 copy-start.6
  9.5 80.1 %reduce-scatter.2.cloned.1.call-start = ((), (), s32[]{:S(2)}) async-start(), calls=%async_computation.2 | async-start | bytes 1114112 | tf_op jit(solution)/shard_map/while/body/eval_jaxpr/reduce_scatter | solution.py:89
  10.0 2.9 copy-start.5
  91.6 20.1 %all-to-all-start = ((bf16[16,8,4096]{2,1,0:T(8,128)(2,1)}), bf16[16,8,4096]{2,1,0:T(8,128)(2,1)S(1)}, u32[]{:S(2)}, u32[]{:S(2)}) async-start(bf16[16,8,4096]{2,1,0:T(8,128)(2,1)} %stack.7), calls=%async_computation.1 | async-start | bytes 2097152 | tf_op jit(solution)/shard_map/while/body/eval_jaxpr/all_to_all | solution.py:123
  95.2 106.4 %all-reduce.2.cloned.1.call-start = ((), (), s32[]{:S(2)}) async-start(), calls=%async_computation.3 | async-start | bytes 2097152 | tf_op jit(solution)/shard_map/while/body/eval_jaxpr/psum | solution.py:18
  112.8 89.1 %collective-permute-start = (bf16[128,4096]{1,0:T(8,128)(2,1)S(1)}, bf16[128,4096]{1,0:T(8,128)(2,1)}, u32[]{:S(2)}, u32[]{:S(2)}) collective-permute-start(bf16[128,4096]{1,0:T(8,128)(2,1)S(1)} %bitcast.89), channel_id=1, source_target_pairs={{0,16},{16,32},{32,48},{48,64},{64,80},{80,96},{96,112},{1,17},{17... | collective-permute-start | bytes 3145736 | tf_op jit(solution)/shard_map/while/body/eval_jaxpr/ppermute | solution.py:13
  119.6 82.3 %copy-start.4 = (f32[4096]{0:T(1024)S(1)}, f32[4096]{0:T(1024)}, u32[]{:S(2)}) copy-start(f32[4096]{0:T(1024)} %get-tuple-element.670) | copy-start | bytes 49156 | tf_op jit(solution)/shard_map/while
  119.6 82.3 %copy-start.7 = (f32[1,4]{1,0:T(1,128)S(1)}, f32[1,4]{1,0:T(1,128)}, u32[]{:S(2)}) copy-start(f32[1,4]{1,0:T(1,128)} %get-tuple-element.696) | copy-start | bytes 52 | tf_op jit(solution)/shard_map/while
  202.0 75.5 %reduce-scatter.2.cloned.1.call-start = ((), (), s32[]{:S(2)}) async-start(), calls=%async_computation.2 | async-start | bytes 1114112 | tf_op jit(solution)/shard_map/while/body/eval_jaxpr/reduce_scatter | solution.py:89
  202.5 2.9 copy-start.5
  279.4 20.1 %all-to-all-start = ((bf16[16,8,4096]{2,1,0:T(8,128)(2,1)}), bf16[16,8,4096]{2,1,0:T(8,128)(2,1)S(1)}, u32[]{:S(2)}, u32[]{:S(2)}) async-start(bf16[16,8,4096]{2,1,0:T(8,128)(2,1)} %stack.7), calls=%async_computation.1 | async-start | bytes 2097152 | tf_op jit(solution)/shard_map/while/body/eval_jaxpr/all_to_all | solution.py:123
  283.0 106.7 %all-reduce.2.cloned.1.call-start = ((), (), s32[]{:S(2)}) async-start(), calls=%async_computation.3 | async-start | bytes 2097152 | tf_op jit(solution)/shard_map/while/body/eval_jaxpr/psum | solution.py:18
  300.6 89.5 %collective-permute-start = (bf16[128,4096]{1,0:T(8,128)(2,1)S(1)}, bf16[128,4096]{1,0:T(8,128)(2,1)}, u32[]{:S(2)}, u32[]{:S(2)}) collective-permute-start(bf16[128,4096]{1,0:T(8,128)(2,1)S(1)} %bitcast.89), channel_id=1, source_target_pairs={{0,16},{16,32},{32,48},{48,64},{64,80},{80,96},{96,112},{1,17},{17... | collective-permute-start | bytes 3145736 | tf_op jit(solution)/shard_map/while/body/eval_jaxpr/ppermute | solution.py:13
  307.3 82.7 %copy-start.4 = (f32[4096]{0:T(1024)S(1)}, f32[4096]{0:T(1024)}, u32[]{:S(2)}) copy-start(f32[4096]{0:T(1024)} %get-tuple-element.670) | copy-start | bytes 49156 | tf_op jit(solution)/shard_map/while
  307.3 82.7 %copy-start.7 = (f32[1,4]{1,0:T(1,128)S(1)}, f32[1,4]{1,0:T(1,128)}, u32[]{:S(2)}) copy-start(f32[1,4]{1,0:T(1,128)} %get-tuple-element.696) | copy-start | bytes 52 | tf_op jit(solution)/shard_map/while
  390.1 75.4 %reduce-scatter.2.cloned.1.call-start = ((), (), s32[]{:S(2)}) async-start(), calls=%async_computation.2 | async-start | bytes 1114112 | tf_op jit(solution)/shard_map/while/body/eval_jaxpr/reduce_scatter | solution.py:89
  390.7 2.9 copy-start.5
  467.4 20.1 %all-to-all-start = ((bf16[16,8,4096]{2,1,0:T(8,128)(2,1)}), bf16[16,8,4096]{2,1,0:T(8,128)(2,1)S(1)}, u32[]{:S(2)}, u32[]{:S(2)}) async-start(bf16[16,8,4096]{2,1,0:T(8,128)(2,1)} %stack.7), calls=%async_computation.1 | async-start | bytes 2097152 | tf_op jit(solution)/shard_map/while/body/eval_jaxpr/all_to_all | solution.py:123
  471.1 106.8 %all-reduce.2.cloned.1.call-start = ((), (), s32[]{:S(2)}) async-start(), calls=%async_computation.3 | async-start | bytes 2097152 | tf_op jit(solution)/shard_map/while/body/eval_jaxpr/psum | solution.py:18
  488.6 90.8 %collective-permute-start = (bf16[128,4096]{1,0:T(8,128)(2,1)S(1)}, bf16[128,4096]{1,0:T(8,128)(2,1)}, u32[]{:S(2)}, u32[]{:S(2)}) collective-permute-start(bf16[128,4096]{1,0:T(8,128)(2,1)S(1)} %bitcast.89), channel_id=1, source_target_pairs={{0,16},{16,32},{32,48},{48,64},{64,80},{80,96},{96,112},{1,17},{17... | collective-permute-start | bytes 3145736 | tf_op jit(solution)/shard_map/while/body/eval_jaxpr/ppermute | solution.py:13
  495.7 83.8 %copy-start.4 = (f32[4096]{0:T(1024)S(1)}, f32[4096]{0:T(1024)}, u32[]{:S(2)}) copy-start(f32[4096]{0:T(1024)} %get-tuple-element.670) | copy-start | bytes 49156 | tf_op jit(solution)/shard_map/while
  495.7 83.8 %copy-start.7 = (f32[1,4]{1,0:T(1,128)S(1)}, f32[1,4]{1,0:T(1,128)}, u32[]{:S(2)}) copy-start(f32[1,4]{1,0:T(1,128)} %get-tuple-element.696) | copy-start | bytes 52 | tf_op jit(solution)/shard_map/while
  579.5 75.4 %reduce-scatter.2.cloned.1.call-start = ((), (), s32[]{:S(2)}) async-start(), calls=%async_computation.2 | async-start | bytes 1114112 | tf_op jit(solution)/shard_map/while/body/eval_jaxpr/reduce_scatter | solution.py:89
  580.0 2.9 copy-start.5
  656.8 20.1 %all-to-all-start = ((bf16[16,8,4096]{2,1,0:T(8,128)(2,1)}), bf16[16,8,4096]{2,1,0:T(8,128)(2,1)S(1)}, u32[]{:S(2)}, u32[]{:S(2)}) async-start(bf16[16,8,4096]{2,1,0:T(8,128)(2,1)} %stack.7), calls=%async_computation.1 | async-start | bytes 2097152 | tf_op jit(solution)/shard_map/while/body/eval_jaxpr/all_to_all | solution.py:123
  660.5 106.6 %all-reduce.2.cloned.1.call-start = ((), (), s32[]{:S(2)}) async-start(), calls=%async_computation.3 | async-start | bytes 2097152 | tf_op jit(solution)/shard_map/while/body/eval_jaxpr/psum | solution.py:18
  678.0 90.6 %collective-permute-start = (bf16[128,4096]{1,0:T(8,128)(2,1)S(1)}, bf16[128,4096]{1,0:T(8,128)(2,1)}, u32[]{:S(2)}, u32[]{:S(2)}) collective-permute-start(bf16[128,4096]{1,0:T(8,128)(2,1)S(1)} %bitcast.89), channel_id=1, source_target_pairs={{0,16},{16,32},{32,48},{48,64},{64,80},{80,96},{96,112},{1,17},{17... | collective-permute-start | bytes 3145736 | tf_op jit(solution)/shard_map/while/body/eval_jaxpr/ppermute | solution.py:13
  685.0 83.6 %copy-start.4 = (f32[4096]{0:T(1024)S(1)}, f32[4096]{0:T(1024)}, u32[]{:S(2)}) copy-start(f32[4096]{0:T(1024)} %get-tuple-element.670) | copy-start | bytes 49156 | tf_op jit(solution)/shard_map/while
  685.0 83.6 %copy-start.7 = (f32[1,4]{1,0:T(1,128)S(1)}, f32[1,4]{1,0:T(1,128)}, u32[]{:S(2)}) copy-start(f32[1,4]{1,0:T(1,128)} %get-tuple-element.696) | copy-start | bytes 52 | tf_op jit(solution)/shard_map/while
  768.7 75.4 %reduce-scatter.2.cloned.1.call-start = ((), (), s32[]{:S(2)}) async-start(), calls=%async_computation.2 | async-start | bytes 1114112 | tf_op jit(solution)/shard_map/while/body/eval_jaxpr/reduce_scatter | solution.py:89
  769.2 2.9 copy-start.5
  846.0 20.1 %all-to-all-start = ((bf16[16,8,4096]{2,1,0:T(8,128)(2,1)}), bf16[16,8,4096]{2,1,0:T(8,128)(2,1)S(1)}, u32[]{:S(2)}, u32[]{:S(2)}) async-start(bf16[16,8,4096]{2,1,0:T(8,128)(2,1)} %stack.7), calls=%async_computation.1 | async-start | bytes 2097152 | tf_op jit(solution)/shard_map/while/body/eval_jaxpr/all_to_all | solution.py:123
  849.7 106.6 %all-reduce.2.cloned.1.call-start = ((), (), s32[]{:S(2)}) async-start(), calls=%async_computation.3 | async-start | bytes 2097152 | tf_op jit(solution)/shard_map/while/body/eval_jaxpr/psum | solution.py:18
  867.2 89.4 %collective-permute-start = (bf16[128,4096]{1,0:T(8,128)(2,1)S(1)}, bf16[128,4096]{1,0:T(8,128)(2,1)}, u32[]{:S(2)}, u32[]{:S(2)}) collective-permute-start(bf16[128,4096]{1,0:T(8,128)(2,1)S(1)} %bitcast.89), channel_id=1, source_target_pairs={{0,16},{16,32},{32,48},{48,64},{64,80},{80,96},{96,112},{1,17},{17... | collective-permute-start | bytes 3145736 | tf_op jit(solution)/shard_map/while/body/eval_jaxpr/ppermute | solution.py:13
  874.3 82.4 %copy-start.4 = (f32[4096]{0:T(1024)S(1)}, f32[4096]{0:T(1024)}, u32[]{:S(2)}) copy-start(f32[4096]{0:T(1024)} %get-tuple-element.670) | copy-start | bytes 49156 | tf_op jit(solution)/shard_map/while
  874.3 82.4 %copy-start.7 = (f32[1,4]{1,0:T(1,128)S(1)}, f32[1,4]{1,0:T(1,128)}, u32[]{:S(2)}) copy-start(f32[1,4]{1,0:T(1,128)} %get-tuple-element.696) | copy-start | bytes 52 | tf_op jit(solution)/shard_map/while
  956.7 75.3 %reduce-scatter.2.cloned.1.call-start = ((), (), s32[]{:S(2)}) async-start(), calls=%async_computation.2 | async-start | bytes 1114112 | tf_op jit(solution)/shard_map/while/body/eval_jaxpr/reduce_scatter | solution.py:89
  957.2 2.9 copy-start.5
  1033.9 20.1 %all-to-all-start = ((bf16[16,8,4096]{2,1,0:T(8,128)(2,1)}), bf16[16,8,4096]{2,1,0:T(8,128)(2,1)S(1)}, u32[]{:S(2)}, u32[]{:S(2)}) async-start(bf16[16,8,4096]{2,1,0:T(8,128)(2,1)} %stack.7), calls=%async_computation.1 | async-start | bytes 2097152 | tf_op jit(solution)/shard_map/while/body/eval_jaxpr/all_to_all | solution.py:123
  1037.6 106.8 %all-reduce.2.cloned.1.call-start = ((), (), s32[]{:S(2)}) async-start(), calls=%async_computation.3 | async-start | bytes 2097152 | tf_op jit(solution)/shard_map/while/body/eval_jaxpr/psum | solution.py:18
  1055.2 89.6 %collective-permute-start = (bf16[128,4096]{1,0:T(8,128)(2,1)S(1)}, bf16[128,4096]{1,0:T(8,128)(2,1)}, u32[]{:S(2)}, u32[]{:S(2)}) collective-permute-start(bf16[128,4096]{1,0:T(8,128)(2,1)S(1)} %bitcast.89), channel_id=1, source_target_pairs={{0,16},{16,32},{32,48},{48,64},{64,80},{80,96},{96,112},{1,17},{17... | collective-permute-start | bytes 3145736 | tf_op jit(solution)/shard_map/while/body/eval_jaxpr/ppermute | solution.py:13
  1062.2 82.6 %copy-start.4 = (f32[4096]{0:T(1024)S(1)}, f32[4096]{0:T(1024)}, u32[]{:S(2)}) copy-start(f32[4096]{0:T(1024)} %get-tuple-element.670) | copy-start | bytes 49156 | tf_op jit(solution)/shard_map/while
  1062.2 82.6 %copy-start.7 = (f32[1,4]{1,0:T(1,128)S(1)}, f32[1,4]{1,0:T(1,128)}, u32[]{:S(2)}) copy-start(f32[1,4]{1,0:T(1,128)} %get-tuple-element.696) | copy-start | bytes 52 | tf_op jit(solution)/shard_map/while
  1144.8 75.4 %reduce-scatter.2.cloned.1.call-start = ((), (), s32[]{:S(2)}) async-start(), calls=%async_computation.2 | async-start | bytes 1114112 | tf_op jit(solution)/shard_map/while/body/eval_jaxpr/reduce_scatter | solution.py:89
  1145.4 2.9 copy-start.5
  1222.1 20.1 %all-to-all-start = ((bf16[16,8,4096]{2,1,0:T(8,128)(2,1)}), bf16[16,8,4096]{2,1,0:T(8,128)(2,1)S(1)}, u32[]{:S(2)}, u32[]{:S(2)}) async-start(bf16[16,8,4096]{2,1,0:T(8,128)(2,1)} %stack.7), calls=%async_computation.1 | async-start | bytes 2097152 | tf_op jit(solution)/shard_map/while/body/eval_jaxpr/all_to_all | solution.py:123
  1225.8 106.8 %all-reduce.2.cloned.1.call-start = ((), (), s32[]{:S(2)}) async-start(), calls=%async_computation.3 | async-start | bytes 2097152 | tf_op jit(solution)/shard_map/while/body/eval_jaxpr/psum | solution.py:18
  1243.4 89.6 %collective-permute-start = (bf16[128,4096]{1,0:T(8,128)(2,1)S(1)}, bf16[128,4096]{1,0:T(8,128)(2,1)}, u32[]{:S(2)}, u32[]{:S(2)}) collective-permute-start(bf16[128,4096]{1,0:T(8,128)(2,1)S(1)} %bitcast.89), channel_id=1, source_target_pairs={{0,16},{16,32},{32,48},{48,64},{64,80},{80,96},{96,112},{1,17},{17... | collective-permute-start | bytes 3145736 | tf_op jit(solution)/shard_map/while/body/eval_jaxpr/ppermute | solution.py:13
  1250.3 82.6 %copy-start.4 = (f32[4096]{0:T(1024)S(1)}, f32[4096]{0:T(1024)}, u32[]{:S(2)}) copy-start(f32[4096]{0:T(1024)} %get-tuple-element.670) | copy-start | bytes 49156 | tf_op jit(solution)/shard_map/while
  1250.4 82.6 %copy-start.7 = (f32[1,4]{1,0:T(1,128)S(1)}, f32[1,4]{1,0:T(1,128)}, u32[]{:S(2)}) copy-start(f32[1,4]{1,0:T(1,128)} %get-tuple-element.696) | copy-start | bytes 52 | tf_op jit(solution)/shard_map/while
  1333.0 75.4 %reduce-scatter.2.cloned.1.call-start = ((), (), s32[]{:S(2)}) async-start(), calls=%async_computation.2 | async-start | bytes 1114112 | tf_op jit(solution)/shard_map/while/body/eval_jaxpr/reduce_scatter | solution.py:89
  1333.5 2.9 copy-start.5
  1410.3 20.1 %all-to-all-start = ((bf16[16,8,4096]{2,1,0:T(8,128)(2,1)}), bf16[16,8,4096]{2,1,0:T(8,128)(2,1)S(1)}, u32[]{:S(2)}, u32[]{:S(2)}) async-start(bf16[16,8,4096]{2,1,0:T(8,128)(2,1)} %stack.7), calls=%async_computation.1 | async-start | bytes 2097152 | tf_op jit(solution)/shard_map/while/body/eval_jaxpr/all_to_all | solution.py:123
  1414.0 106.7 %all-reduce.2.cloned.1.call-start = ((), (), s32[]{:S(2)}) async-start(), calls=%async_computation.3 | async-start | bytes 2097152 | tf_op jit(solution)/shard_map/while/body/eval_jaxpr/psum | solution.py:18
  1431.5 89.4 %collective-permute-start = (bf16[128,4096]{1,0:T(8,128)(2,1)S(1)}, bf16[128,4096]{1,0:T(8,128)(2,1)}, u32[]{:S(2)}, u32[]{:S(2)}) collective-permute-start(bf16[128,4096]{1,0:T(8,128)(2,1)S(1)} %bitcast.89), channel_id=1, source_target_pairs={{0,16},{16,32},{32,48},{48,64},{64,80},{80,96},{96,112},{1,17},{17... | collective-permute-start | bytes 3145736 | tf_op jit(solution)/shard_map/while/body/eval_jaxpr/ppermute | solution.py:13
  1438.4 82.6 %copy-start.4 = (f32[4096]{0:T(1024)S(1)}, f32[4096]{0:T(1024)}, u32[]{:S(2)}) copy-start(f32[4096]{0:T(1024)} %get-tuple-element.670) | copy-start | bytes 49156 | tf_op jit(solution)/shard_map/while
  1438.4 82.6 %copy-start.7 = (f32[1,4]{1,0:T(1,128)S(1)}, f32[1,4]{1,0:T(1,128)}, u32[]{:S(2)}) copy-start(f32[1,4]{1,0:T(1,128)} %get-tuple-element.696) | copy-start | bytes 52 | tf_op jit(solution)/shard_map/while
  1521.0 75.4 %reduce-scatter.2.cloned.1.call-start = ((), (), s32[]{:S(2)}) async-start(), calls=%async_computation.2 | async-start | bytes 1114112 | tf_op jit(solution)/shard_map/while/body/eval_jaxpr/reduce_scatter | solution.py:89
  1521.6 2.9 copy-start.5
  1598.4 20.1 %all-to-all-start = ((bf16[16,8,4096]{2,1,0:T(8,128)(2,1)}), bf16[16,8,4096]{2,1,0:T(8,128)(2,1)S(1)}, u32[]{:S(2)}, u32[]{:S(2)}) async-start(bf16[16,8,4096]{2,1,0:T(8,128)(2,1)} %stack.7), calls=%async_computation.1 | async-start | bytes 2097152 | tf_op jit(solution)/shard_map/while/body/eval_jaxpr/all_to_all | solution.py:123
  1602.1 106.8 %all-reduce.2.cloned.1.call-start = ((), (), s32[]{:S(2)}) async-start(), calls=%async_computation.3 | async-start | bytes 2097152 | tf_op jit(solution)/shard_map/while/body/eval_jaxpr/psum | solution.py:18
  1619.6 89.6 %collective-permute-start = (bf16[128,4096]{1,0:T(8,128)(2,1)S(1)}, bf16[128,4096]{1,0:T(8,128)(2,1)}, u32[]{:S(2)}, u32[]{:S(2)}) collective-permute-start(bf16[128,4096]{1,0:T(8,128)(2,1)S(1)} %bitcast.89), channel_id=1, source_target_pairs={{0,16},{16,32},{32,48},{48,64},{64,80},{80,96},{96,112},{1,17},{17... | collective-permute-start | bytes 3145736 | tf_op jit(solution)/shard_map/while/body/eval_jaxpr/ppermute | solution.py:13
  1626.6 82.6 %copy-start.4 = (f32[4096]{0:T(1024)S(1)}, f32[4096]{0:T(1024)}, u32[]{:S(2)}) copy-start(f32[4096]{0:T(1024)} %get-tuple-element.670) | copy-start | bytes 49156 | tf_op jit(solution)/shard_map/while
  1626.6 82.6 %copy-start.7 = (f32[1,4]{1,0:T(1,128)S(1)}, f32[1,4]{1,0:T(1,128)}, u32[]{:S(2)}) copy-start(f32[1,4]{1,0:T(1,128)} %get-tuple-element.696) | copy-start | bytes 52 | tf_op jit(solution)/shard_map/while
  (20 other events, 33.2 us)
Sparse Core Ops, SparseCore 0:
  24.6 65.0 reduce-scatter.1
  112.9 88.6 all-reduce.1
  217.0 60.3 reduce-scatter.1
  300.7 88.9 all-reduce.1
  405.2 60.2 reduce-scatter.1
  488.7 89.0 all-reduce.1
  594.6 60.2 reduce-scatter.1
  678.1 88.9 all-reduce.1
  783.8 60.2 reduce-scatter.1
  867.3 88.9 all-reduce.1
  971.8 60.1 reduce-scatter.1
  1055.3 89.1 all-reduce.1
  1159.9 60.2 reduce-scatter.1
  1243.5 89.0 all-reduce.1
  1348.0 60.2 reduce-scatter.1
  1431.6 88.9 all-reduce.1
  1536.1 60.2 reduce-scatter.1
  1619.7 89.0 all-reduce.1
